TPU v7x, 32 devices: a whole 2x2x4 slice. The times are simulated.
32 devices in a mesh: inl: 4 (over x, core), xl: 8 (over z, y).
Axes of the slice: x: 2, y: 2, z: 4, core: 2. Of those that a mesh axis runs over, the one named last changes fastest.
Arguments:
- baseline: float32 [16, 128, 1024], P('inl', 'xl'), may hold values from -600 to 600
- monitor: float32 [16, 128, 1024], P('inl', 'xl'), may hold values from -900 to 900
- shift_model: float32 [4, 32, 128], P(None, None, 'xl'), may hold values from -4 to 4
- knot_start: int32 [32, 4], replicated, may hold values from -12 to 13, as said below
- half_width: int32 [8], P('xl'), may hold values from 1 to 3
Outputs:
- shift_obs: float32 [16, 128, 1024], P('inl', 'xl')
- delta: float32 [4, 32, 128], P(None, 'xl', 'inl')
Inputs may be any that keep to these rules, and one draw needn't show every extreme that they name: `knot_start`: basis function k of a window starts at sample k * 8 - 3 * 4 or one later, relative to the window's first sample.
All inputs are finite; a program needn't handle non-finite values.
Results may differ from a plain program's by a relative error of at most 0.00018.
Values sent between devices are 32-bit elements; how exact they have to be, the bound alone decides.
A program may use at most 64 MiB of HBM per device.

v0:
```python
import jax
import jax.numpy as jnp
from jax import lax
from jax.sharding import PartitionSpec as P

LAGS = 15
TWIN = 12
HMAX = 3
WINLEN = 32
KW = 4
KSTEP = 8
EPSILON = 1e-06
SHARPNESS = 6.0
DAMPING = 0.5


def extended(block, sides, width):
    for axis, dim in sides:
        count = lax.axis_size(axis)
        forward = [(i, i + 1) for i in range(count - 1)]
        backward = [(target, source) for source, target in forward]
        low = lax.ppermute(
            lax.slice_in_dim(block, block.shape[dim] - width, None, axis=dim), axis, forward
        )
        high = lax.ppermute(lax.slice_in_dim(block, 0, width, axis=dim), axis, backward)
        block = jnp.concatenate([low, block, high], axis=dim)
    return block


def spline(offset):
    square = offset * offset
    cubed = square * offset
    piece_one = cubed / 6.0
    piece_two = (-3.0 * cubed + 12.0 * square - 12.0 * offset + 4.0) / 6.0
    piece_three = (3.0 * cubed - 24.0 * square + 60.0 * offset - 44.0) / 6.0
    remain = 4.0 - offset
    piece_four = remain * remain * remain / 6.0
    result = jnp.where(offset < 4.0, piece_four, 0.0 * offset)
    result = jnp.where(offset < 3.0, piece_three, result)
    result = jnp.where(offset < 2.0, piece_two, result)
    result = jnp.where(offset < 1.0, piece_one, result)
    return jnp.where(offset < 0.0, 0.0 * offset, result)


def basis_table(knot_start):
    positions = jnp.arange(WINLEN).astype(jnp.float32)
    offset = (positions[None, None, :] - knot_start[:, :, None].astype(jnp.float32)) / KSTEP
    return spline(offset)


def solve_small(matrix, target):
    lower = [[None] * KW for _ in range(KW)]
    for column in range(KW):
        pivot = matrix[column][column]
        for inner in range(column):
            pivot = pivot - lower[column][inner] * lower[column][inner]
        lower[column][column] = jnp.sqrt(pivot)
        for target_row in range(column + 1, KW):
            entry = matrix[target_row][column]
            for inner in range(column):
                entry = entry - lower[target_row][inner] * lower[column][inner]
            lower[target_row][column] = entry / lower[column][column]
    forward = []
    for column in range(KW):
        entry = target[column]
        for inner in range(column):
            entry = entry - lower[column][inner] * forward[inner]
        forward.append(entry / lower[column][column])
    backward = [None] * KW
    for column in range(KW - 1, -1, -1):
        entry = forward[column]
        for inner in range(column + 1, KW):
            entry = entry - lower[inner][column] * backward[inner]
        backward[column] = entry / lower[column][column]
    return jnp.stack(backward)


def box_time(values):
    samples = values.shape[2]
    width = 2 * TWIN + 1
    padded = jnp.pad(values, ((0, 0), (0, 0), (TWIN, TWIN)))
    partial_sums = {1: padded}
    length = 1
    while 2 * length <= width:
        previous = partial_sums[length]
        partial_sums[2 * length] = previous[:, :, :-length] + previous[:, :, length:]
        length = 2 * length
    total = None
    begin = 0
    remain = width
    while remain > 0:
        if length <= remain:
            piece = partial_sums[length][:, :, begin : begin + samples]
            total = piece if total is None else total + piece
            begin = begin + length
            remain = remain - length
        length = length // 2
    return total


def normal_terms(resid_four, conf_four, table):
    row_count = resid_four.shape[0]
    windows = resid_four.shape[2]
    crossl = resid_four.shape[1]
    grad = jnp.einsum(
        "ixwu,wku->ikwx", conf_four * resid_four, table, precision=lax.Precision.HIGHEST
    )
    hess = jnp.einsum(
        "ixwu,wku,wju->ikjwx", conf_four, table, table, precision=lax.Precision.HIGHEST
    )
    return jnp.concatenate([grad, hess.reshape(row_count, KW * KW, windows, crossl)], axis=1)


def per_device(baseline, monitor, shift_model, knot_start, half_width):
    inline_rows = baseline.shape[0]
    slab_width = baseline.shape[1]
    samples = baseline.shape[2]
    paired = extended(jnp.stack([baseline, monitor]), (("xl", 2),), HMAX)
    base_ext = paired[0]
    moni_ext = paired[1]
    half_span = half_width[0]
    lateral = [
        (jnp.abs(offset) <= half_span).astype(jnp.float32) for offset in range(-HMAX, HMAX + 1)
    ]

    def smooth(values):
        timed = box_time(values)
        total = None
        for place, offset in enumerate(range(-HMAX, HMAX + 1)):
            term = lateral[place] * timed[:, HMAX + offset : HMAX + offset + slab_width]
            total = term if total is None else total + term
        return total

    energy_base = smooth(base_ext * base_ext)
    moni_pad = jnp.pad(moni_ext, ((0, 0), (0, 0), (LAGS, LAGS)))
    energy_mon = smooth(moni_pad * moni_pad)

    def one_lag(lag_index, running):
        total_exp, total_shift, total_corr = running
        lagged = lax.dynamic_slice_in_dim(moni_pad, lag_index, samples, 2)
        correlation = smooth(base_ext * lagged)
        energy = lax.dynamic_slice_in_dim(energy_mon, lag_index, samples, 2)
        normed = correlation / jnp.sqrt(energy_base * energy + EPSILON)
        weight_exp = jnp.exp(SHARPNESS * normed)
        lag_value = jnp.asarray(lag_index - LAGS, jnp.int32).astype(jnp.float32)
        return (
            total_exp + weight_exp,
            total_shift + lag_value * weight_exp,
            total_corr + normed * weight_exp,
        )

    first_lag = one_lag(0, (0.0 * energy_base, 0.0 * energy_base, 0.0 * energy_base))
    total_exp, total_shift, total_corr = lax.fori_loop(1, 2 * LAGS + 1, one_lag, first_lag)
    shift_obs = total_shift / total_exp
    confidence = 0.5 + 0.5 * total_corr / total_exp
    table = basis_table(knot_start)
    modelled = jnp.einsum(
        "kwx,wku->xwu", shift_model, table, precision=lax.Precision.HIGHEST
    ).reshape(slab_width, samples)
    resid = shift_obs - modelled[None]
    resid_piece = lax.all_to_all(resid, "xl", split_axis=2, concat_axis=1, tiled=True)
    conf_piece = lax.all_to_all(confidence, "xl", split_axis=2, concat_axis=1, tiled=True)
    row_count = resid_piece.shape[0]
    crossl = resid_piece.shape[1]
    owned = resid_piece.shape[2] // WINLEN
    table_own = lax.dynamic_slice_in_dim(table, lax.axis_index("xl") * owned, owned, 0)
    resid_four = resid_piece.reshape(row_count, crossl, owned, WINLEN)
    conf_four = conf_piece.reshape(row_count, crossl, owned, WINLEN)
    per_row = normal_terms(resid_four, conf_four, table_own)
    normal = jnp.sum(per_row, axis=0)
    summed = lax.psum(normal, "inl")
    share = summed.shape[2] // lax.axis_size("inl")
    summed = lax.dynamic_slice_in_dim(summed, lax.axis_index("inl") * share, share, 2)
    damping = DAMPING * inline_rows * lax.axis_size("inl")
    matrix = [
        [
            summed[KW + KW * first_k + second_k] + (damping if first_k == second_k else 0.0)
            for second_k in range(KW)
        ]
        for first_k in range(KW)
    ]
    target = [summed[first_k] for first_k in range(KW)]
    delta = solve_small(matrix, target)
    return (shift_obs, delta)


def solution(mesh):
    in_specs = (P("inl", "xl", None), P("inl", "xl", None), P(None, None, "xl"), P(), P("xl"))
    out_specs = (P("inl", "xl", None), P(None, "xl", "inl"))
    return jax.shard_map(
        per_device, mesh=mesh, in_specs=in_specs, out_specs=out_specs, check_vma=False
    )
```

profile of v0, /device:TPU:0, one launch (start us, length us, event | category | flops | bytes accessed | tf_op | source)
XLA Modules:
  0.0 127.3 jit_solution(12901075774814896960)
XLA Ops:
  0.6 1.2 pad_maximum_fusion.2
  1.9 1.3 %collective-permute-start.1 = (f32[2,4,3,1024]{3,2,1,0:T(4,128)S(1)}, f32[2,4,3,1024]{3,2,1,0:T(4,128)S(1)}, u32[]{:S(2)}, u32[]{:S(2)}) collective-permute-start(f32[2,4,3,1024]{3,2,1,0:T(4,128)S(1)} %get-tuple-element.489), channel_id=1, source_target_pairs={{1,0},{2,1},{3,2},{4,3},{5,4},{6,5},{7,6},{9,8},{10,9},{11,10},{12... | collective-permute-start | bytes 294920 | tf_op jit(solution)/shard_map/ppermute | solution.py:25
  3.2 5.5 %collective-permute-start = (f32[2,4,3,1024]{3,2,1,0:T(4,128)S(1)}, f32[2,4,3,1024]{3,2,1,0:T(4,128)S(1)}, u32[]{:S(2)}, u32[]{:S(2)}) collective-permute-start(f32[2,4,3,1024]{3,2,1,0:T(4,128)S(1)} %get-tuple-element.488), channel_id=1, source_target_pairs={{0,1},{1,2},{2,3},{3,4},{4,5},{5,6},{6,7},{8,9},{9,10},{10,11},{11... | collective-permute-start | bytes 294920 | tf_op jit(solution)/shard_map/ppermute | solution.py:22
  8.7 0.8 copy.41
  9.5 0.7 convert_element_type.72
  10.3 0.8 convolution_bitcast_fusion
  12.0 1.2 collective-permute-done
  14.6 0.5 slice_add_fusion.14
  17.4 0.5 multiply_add_fusion.2
  18.0 56.6 %while.21 = (s32[]{:T(128)}, f32[4,16,1024]{2,1,0:T(8,128)S(1)}, f32[4,16,1024]{2,1,0:T(8,128)S(1)}, f32[4,16,1024]{2,1,0:T(8,128)S(1)}, f32[]{:T(128)}, /*index...) while((s32[]{:T(128)}, f32[4,16,1024]{2,1,0:T(8,128)S(1)}, ...), condition=%wide.region_1.2_spmd, body=%wide.region_0.1_spmd.sunk | while | flops 2143487 | bytes 11726543 | solution.py:153
  19.3 0.4 multiply_add_fusion.6
  21.2 0.4 multiply_add_fusion.6
  23.1 0.4 multiply_add_fusion.6
  25.0 0.4 multiply_add_fusion.6
  26.9 0.4 multiply_add_fusion.6
  28.7 0.4 multiply_add_fusion.6
  30.6 0.4 multiply_add_fusion.6
  32.5 0.4 multiply_add_fusion.6
  34.4 0.4 multiply_add_fusion.6
  38.2 0.4 multiply_add_fusion.6
  47.6 0.4 multiply_add_fusion.6
  51.4 0.4 multiply_add_fusion.6
  60.8 0.4 multiply_add_fusion.6
  74.0 0.4 multiply_add_fusion.6
  74.6 1.7 %copy.36 = f32[4,16,1024]{1,0,2:T(4,128)} copy(f32[4,16,1024]{2,1,0:T(8,128)S(1)} %get-tuple-element.429) | data formatting | bytes 524288 | tf_op jit(solution)/shard_map/while | solution.py:153
  76.3 1.7 %copy.37 = f32[4,16,1024]{1,0,2:T(4,128)} copy(f32[4,16,1024]{2,1,0:T(8,128)S(1)} %get-tuple-element.430) | data formatting | bytes 524288 | tf_op jit(solution)/shard_map/while | solution.py:153
  78.1 0.8 copy.39
  78.9 2.3 %reshape.48 = f32[8,1,8192]{2,1,0:T(1,128)} reshape(f32[1024,4,16]{2,1,0:T(4,128)S(1)} %bitcast.52) | data formatting | bytes 524288
  81.2 6.1 %all-to-all-start = ((f32[8,1,8192]{2,1,0:T(1,128)}), f32[8,1,8192]{2,1,0:T(1,128)S(1)}, u32[]{:S(2)}, u32[]{:S(2)}) async-start(f32[8,1,8192]{2,1,0:T(1,128)} %reshape.48), calls=%async_computation | async-start | bytes 524288 | tf_op jit(solution)/shard_map/all_to_all | solution.py:162
  87.3 4.4 %broadcast_subtract_fusion = (f32[4,16,1024]{1,0,2:T(4,128)}, f32[4,16,1024]{1,0,2:T(4,128)S(1)}) fusion(f32[16,1024]{0,1:T(8,128)S(1)} %bitcast.55, f32[4,16,1024]{1,0,2:T(4,128)} %copy.36, f32[4,16,1024]{1,0,2:T(4,128)} %copy.37), kind=kLoop, calls=%fused_computation.31 | loop fusion | flops 131072 | bytes 1114112 | tf_op jit(solution)/shard_map/sub | solution.py:160
  91.7 3.8 %reshape.50 = f32[8,1,8192]{2,1,0:T(1,128)} reshape(f32[1024,4,16]{2,1,0:T(4,128)} %bitcast.51) | data formatting | bytes 524288
  95.5 0.6 all-to-all-done
  96.1 5.4 %all-to-all-start.1 = ((f32[8,1,8192]{2,1,0:T(1,128)}), f32[8,1,8192]{2,1,0:T(1,128)S(1)}, u32[]{:S(2)}, u32[]{:S(2)}) async-start(f32[8,1,8192]{2,1,0:T(1,128)} %reshape.50), calls=%async_computation.1 | async-start | bytes 524288 | tf_op jit(solution)/shard_map/all_to_all | solution.py:161
  101.7 1.4 %copy.50 = f32[4,16,1024]{2,1,0:T(8,128)} copy(f32[4,16,1024]{1,0,2:T(4,128)S(1)} %get-tuple-element.474) | data formatting | bytes 524288
  103.2 0.5 broadcast.174
  103.7 1.3 reduce
  105.0 1.5 %reshape.49 = f32[1024,4,16]{2,1,0:T(4,128)S(1)} reshape(f32[8,8192]{1,0:T(8,128)S(1)} %reduce) | data formatting | bytes 524288
  106.5 0.8 copy.40
  107.2 0.5 reshape.38
  107.7 1.0 convolution_bitcast_fusion.1
  108.7 1.1 all-to-all-done.1
  109.9 1.3 reduce.1
  111.1 1.5 %reshape.51 = f32[1024,4,16]{2,1,0:T(4,128)S(1)} reshape(f32[8,8192]{1,0:T(8,128)S(1)} %reduce.1) | data formatting | bytes 524288
  112.7 0.8 copy.44
  113.4 0.5 reshape.39
  114.2 1.6 %convolution_bitcast_fusion.2 = f32[4,4,4,128]{3,1,0,2:T(4,128)S(1)} fusion(f32[4,128,4,32]{3,2,1,0:T(4,128)S(1)} %mul.591, f32[32,4,32]{2,1,0:T(4,128)} %copy-done.2, s32[]{:T(128)S(6)} %select_n.40), kind=kOutput, calls=%fused_computation.28 | convolution fusion | flops 3145728 | bytes 303108 | tf_op jit(solution)/shard_map/ixwu,wku->ikwx/dot_general | solution.py:105
  115.9 10.5 %psum.7 = f32[20,4,128]{2,1,0:T(4,128)S(1)} all-reduce(f32[20,4,128]{2,1,0:T(4,128)S(1)} %copy.49), channel_id=1, replica_groups=mesh['inl'=4,'xl'=8] {'inl'}, use_global_device_ids=true, to_apply=%region_3.4 | all-reduce | flops 10240 | bytes 81920 | tf_op jit(solution)/shard_map/psum | solution.py:171
  126.7 0.6 pad_maximum_fusion.3
  (265 shorter events, 54.1 us)
Async XLA Ops:
  0.6 12.6 %copy-start = (f32[4,16,1024]{2,1,0:T(8,128)S(1)}, f32[4,16,1024]{2,1,0:T(8,128)}, u32[]{:S(2)}) copy-start(f32[4,16,1024]{2,1,0:T(8,128)} %param.8) | copy-start | bytes 786436
  0.6 12.6 %copy-start.1 = (f32[4,16,1024]{2,1,0:T(8,128)S(1)}, f32[4,16,1024]{2,1,0:T(8,128)}, u32[]{:S(2)}) copy-start(f32[4,16,1024]{2,1,0:T(8,128)} %param.7) | copy-start | bytes 786436
  1.9 10.1 %collective-permute-start.1 = (f32[2,4,3,1024]{3,2,1,0:T(4,128)S(1)}, f32[2,4,3,1024]{3,2,1,0:T(4,128)S(1)}, u32[]{:S(2)}, u32[]{:S(2)}) collective-permute-start(f32[2,4,3,1024]{3,2,1,0:T(4,128)S(1)} %get-tuple-element.489), channel_id=1, source_target_pairs={{1,0},{2,1},{3,2},{4,3},{5,4},{6,5},{7,6},{9,8},{10,9},{11,10},{12... | collective-permute-start | bytes 294920 | tf_op jit(solution)/shard_map/ppermute | solution.py:25
  3.2 10.0 %collective-permute-start = (f32[2,4,3,1024]{3,2,1,0:T(4,128)S(1)}, f32[2,4,3,1024]{3,2,1,0:T(4,128)S(1)}, u32[]{:S(2)}, u32[]{:S(2)}) collective-permute-start(f32[2,4,3,1024]{3,2,1,0:T(4,128)S(1)} %get-tuple-element.488), channel_id=1, source_target_pairs={{0,1},{1,2},{2,3},{3,4},{4,5},{5,6},{6,7},{8,9},{9,10},{10,11},{11... | collective-permute-start | bytes 294920 | tf_op jit(solution)/shard_map/ppermute | solution.py:22
  81.2 14.9 %all-to-all-start = ((f32[8,1,8192]{2,1,0:T(1,128)}), f32[8,1,8192]{2,1,0:T(1,128)S(1)}, u32[]{:S(2)}, u32[]{:S(2)}) async-start(f32[8,1,8192]{2,1,0:T(1,128)} %reshape.48), calls=%async_computation | async-start | bytes 524288 | tf_op jit(solution)/shard_map/all_to_all | solution.py:162
  96.1 13.8 %all-to-all-start.1 = ((f32[8,1,8192]{2,1,0:T(1,128)}), f32[8,1,8192]{2,1,0:T(1,128)S(1)}, u32[]{:S(2)}, u32[]{:S(2)}) async-start(f32[8,1,8192]{2,1,0:T(1,128)} %reshape.50), calls=%async_computation.1 | async-start | bytes 524288 | tf_op jit(solution)/shard_map/all_to_all | solution.py:161
  101.7 1.5 %copy-start.2 = (f32[32,4,32]{2,1,0:T(4,128)}, f32[32,4,32]{2,1,0:T(4,128)S(1)}, u32[]{:S(2)}) copy-start(f32[32,4,32]{2,1,0:T(4,128)S(1)} %fusion.46) | copy-start | bytes 49156
where the time goes:
time: 128 us; the launch traced here: 127 us
  other arithmetic  63.6 us (50%)
  local copies, waits for them, and re-layouts  24.9 us (19%)
  starting transfers between devices  18.3 us (14%)
  blocking collectives  10.5 us (8%)
  matrix products  3.41 us (3%)
  waiting for transfers between devices  2.93 us (2%)
  loops' own time  2.02 us (2%)
  between operations  1.66 us (1%)
    add x98, other arithmetic, box_time(): previous[:, :, :-length] + previous[:, :, length:]  21.5 us
    add x31, other arithmetic, one_lag(): total_corr + normed * weight_exp  12 us
    unnamed x12, local copies, waits for them, and re-layouts  11.3 us
    psum x1, blocking collectives, per_device(): summed = lax.psum(normal, 'inl')  10.5 us
    add x33, other arithmetic, box_time(): total = piece if total is None else total + piece  9.07 us
    all_to_all x1, starting transfers between devices, per_device(): lax.all_to_all(confidence, 'xl', split_axis=2, concat_axis=1, tiled=True)  6.08 us
    slice x33, local copies, waits for them, and re-layouts, box_time(): previous[:, :, :-length] + previous[:, :, length:]  5.94 us
    ppermute x1, starting transfers between devices, extended(): lax.ppermute(lax.slice_in_dim(block, block.shape[dim] - width, None, axis...  5.51 us
  transfers between devices with their start and end apart: 4, of which 3 were waited for; matrix products, arithmetic and copies ran while one was open for 14% of the time, Pallas kernels for 0%

commit v1 on v0

--- a/solution.py
+++ b/solution.py
@@ -12,6 +12,17 @@
 EPSILON = 1e-06
 SHARPNESS = 6.0
 DAMPING = 0.5
+
+
+def in_blocks(value, dim, size):
+    before, after = (value.shape[:dim], value.shape[dim + 1 :])
+    return jnp.moveaxis(value.reshape(*before, size, -1, *after), dim, 0)
+
+
+def laid_out(blocks, dim):
+    lengths = list(blocks.shape[1:])
+    lengths[dim] *= blocks.shape[0]
+    return jnp.moveaxis(blocks, 0, dim).reshape(lengths)
 
 
 def extended(block, sides, width):
@@ -158,7 +169,14 @@
         "kwx,wku->xwu", shift_model, table, precision=lax.Precision.HIGHEST
     ).reshape(slab_width, samples)
     resid = shift_obs - modelled[None]
-    resid_piece = lax.all_to_all(resid, "xl", split_axis=2, concat_axis=1, tiled=True)
+    count_2, index = (lax.axis_size("xl"), lax.axis_index("xl"))
+    blocks = in_blocks(resid, 2, count_2)
+    done = [blocks[index]]
+    for step in range(1, count_2):
+        sent = blocks[index ^ step]
+        done.append(lax.ppermute(sent, "xl", [(i_2, i_2 ^ step) for i_2 in range(count_2)]))
+    blocks = jnp.stack(done)[index ^ jnp.arange(count_2)]
+    resid_piece = laid_out(blocks, 1)
     conf_piece = lax.all_to_all(confidence, "xl", split_axis=2, concat_axis=1, tiled=True)
     row_count = resid_piece.shape[0]
     crossl = resid_piece.shape[1]

time: 128 us -> 122 us (0.953)
  local copies, waits for them, and re-layouts: 24.9 us -> 14.9 us
  starting transfers between devices: 18.3 us -> 24.2 us
  other arithmetic: 63.6 us -> 58.7 us
  waiting for transfers between devices: 2.93 us -> 7.08 us
    ppermute x0 -> x7, starting transfers between devices: none -> 13.6 us  [per_device(): lax.ppermute(sent, 'xl', [(i_2, i_2 ^ step) for i_2 in range(count_2)])]
    unnamed x12 -> x15, local copies, waits for them, and re-layouts: 11.3 us -> 4.7 us
    all_to_all x1 -> x0, starting transfers between devices: 5.39 us -> none  [per_device(): lax.all_to_all(resid, 'xl', split_axis=2, concat_axis=1, tiled=True)]
    ppermute x0 -> x7, waiting for transfers between devices: none -> 5.19 us  [per_device(): lax.ppermute(sent, 'xl', [(i_2, i_2 ^ step) for i_2 in range(count_2)])]
    sub x1, other arithmetic: 4.44 us -> 0.81 us  [per_device(): resid = shift_obs - modelled[None]]
    while x2 -> x0, local copies, waits for them, and re-layouts: 3.44 us -> none  [per_device(): lax.fori_loop(1, 2 * LAGS + 1, one_lag, first_lag)]
    ppermute x1, waiting for transfers between devices: 0.01 us -> 1.88 us  [extended(): lax.ppermute(lax.slice_in_dim(block, 0, width, axis=dim), axis, backward)]
    all_to_all x1, starting transfers between devices: 6.08 us -> 4.46 us  [per_device(): lax.all_to_all(confidence, 'xl', split_axis=2, concat_axis=1, tiled=True)]
  transfers between devices with their start and end apart: 4 -> 10, of which waited for: 3 -> 3; matrix products, arithmetic and copies ran while one was open for 14% -> 6% of each run, Pallas kernels for 0% -> 0%
where the time goes in v1:
time: 122 us
  other arithmetic  58.7 us (48%)
  starting transfers between devices  24.2 us (20%)
  local copies, waits for them, and re-layouts  14.9 us (12%)
  blocking collectives  10.5 us (9%)
  waiting for transfers between devices  7.08 us (6%)
  matrix products  2.73 us (2%)
  loops' own time  2.02 us (2%)
  between operations  1.77 us (1%)
    add x98, other arithmetic, box_time(): previous[:, :, :-length] + previous[:, :, length:]  21.5 us
    ppermute x7, starting transfers between devices, per_device(): lax.ppermute(sent, 'xl', [(i_2, i_2 ^ step) for i_2 in range(count_2)])  13.6 us
    add x31, other arithmetic, one_lag(): total_corr + normed * weight_exp  12 us
    psum x1, blocking collectives, per_device(): summed = lax.psum(normal, 'inl')  10.5 us
    add x33, other arithmetic, box_time(): total = piece if total is None else total + piece  9.07 us
    slice x33, local copies, waits for them, and re-layouts, box_time(): previous[:, :, :-length] + previous[:, :, length:]  5.94 us
    mul x30, other arithmetic, one_lag(): correlation = smooth(base_ext * lagged)  5.19 us
    ppermute x7, waiting for transfers between devices, per_device(): lax.ppermute(sent, 'xl', [(i_2, i_2 ^ step) for i_2 in range(count_2)])  5.19 us
  transfers between devices with their start and end apart: 10, of which 3 were waited for; matrix products, arithmetic and copies ran while one was open for 6% of the time, Pallas kernels for 0%

profile of v1, /device:TPU:0, one launch (start us, length us, event | category | flops | bytes accessed | tf_op | source)
XLA Modules:
  0.0 121.9 jit_solution(16617222505488802014)
XLA Ops:
  0.6 1.2 pad_maximum_fusion.2
  1.9 4.9 %collective-permute-start = (f32[2,4,3,1024]{3,2,1,0:T(4,128)S(1)}, f32[2,4,3,1024]{3,2,1,0:T(4,128)S(1)}, u32[]{:S(2)}, u32[]{:S(2)}) collective-permute-start(f32[2,4,3,1024]{3,2,1,0:T(4,128)S(1)} %get-tuple-element.486), channel_id=1, source_target_pairs={{0,1},{1,2},{2,3},{3,4},{4,5},{5,6},{6,7},{8,9},{9,10},{10,11},{11... | collective-permute-start | bytes 294920 | tf_op jit(solution)/shard_map/ppermute | solution.py:33
  6.7 1.3 %collective-permute-start.1 = (f32[2,4,3,1024]{3,2,1,0:T(4,128)S(1)}, f32[2,4,3,1024]{3,2,1,0:T(4,128)S(1)}, u32[]{:S(2)}, u32[]{:S(2)}) collective-permute-start(f32[2,4,3,1024]{3,2,1,0:T(4,128)S(1)} %get-tuple-element.487), channel_id=1, source_target_pairs={{1,0},{2,1},{3,2},{4,3},{5,4},{6,5},{7,6},{9,8},{10,9},{11,10},{12... | collective-permute-start | bytes 294920 | tf_op jit(solution)/shard_map/ppermute | solution.py:36
  8.8 0.7 convert_element_type.72
  9.5 0.8 copy.59
  10.6 0.8 convolution_bitcast_fusion
  11.7 1.9 %collective-permute-done.1 = f32[2,4,3,1024]{3,2,1,0:T(4,128)S(1)} collective-permute-done((f32[2,4,3,1024]{3,2,1,0:T(4,128)S(1)}, f32[2,4,3,1024]{3,2,1,0:T(4,128)S(1)}, u32[]{:S(2)}, u32[]{:S(2)}) %collective-permute-start.1) | collective-permute-done | bytes 98336 | tf_op jit(solution)/shard_map/ppermute | solution.py:36
  14.2 0.5 slice_add_fusion.14
  17.8 0.5 multiply_add_fusion.2
  18.4 56.6 %while.21 = (s32[]{:T(128)}, f32[4,16,1024]{2,1,0:T(8,128)S(1)}, f32[4,16,1024]{2,1,0:T(8,128)S(1)}, f32[4,16,1024]{2,1,0:T(8,128)S(1)}, f32[]{:T(128)}, /*index...) while((s32[]{:T(128)}, f32[4,16,1024]{2,1,0:T(8,128)S(1)}, ...), condition=%wide.region_1.2_spmd, body=%wide.region_0.1_spmd.sunk | while | flops 2143487 | bytes 11726543 | solution.py:164
  19.7 0.4 multiply_add_fusion.6
  21.6 0.4 multiply_add_fusion.6
  23.5 0.4 multiply_add_fusion.6
  25.4 0.4 multiply_add_fusion.6
  27.3 0.4 multiply_add_fusion.6
  29.2 0.4 multiply_add_fusion.6
  31.1 0.4 multiply_add_fusion.6
  32.9 0.4 multiply_add_fusion.6
  34.8 0.4 multiply_add_fusion.6
  36.7 0.4 multiply_add_fusion.6
  38.6 0.4 multiply_add_fusion.6
  49.9 0.4 multiply_add_fusion.6
  59.4 0.4 multiply_add_fusion.6
  63.1 0.4 multiply_add_fusion.6
  72.6 0.4 multiply_add_fusion.6
  75.0 0.8 broadcast_subtract_fusion
  76.1 2.5 %collective-permute-start.2 = (f32[4,16,128]{2,1,0:T(8,128)S(1)}, f32[4,16,128]{2,1,0:T(8,128)S(1)}, u32[]{:S(2)}, u32[]{:S(2)}) collective-permute-start(f32[4,16,128]{2,1,0:T(8,128)S(1)} %bitcast.109), channel_id=1, source_target_pairs={{0,1},{1,0},{2,3},{3,2},{4,5},{5,4},{6,7},{7,6},{8,9},{9,8},{10,11... | collective-permute-start | bytes 98312 | tf_op jit(solution)/shard_map/ppermute | solution.py:177
  78.6 1.6 %collective-permute-start.3 = (f32[4,16,128]{2,1,0:T(8,128)S(1)}, f32[4,16,128]{2,1,0:T(8,128)S(1)}, u32[]{:S(2)}, u32[]{:S(2)}) collective-permute-start(f32[4,16,128]{2,1,0:T(8,128)S(1)} %bitcast.108), channel_id=1, source_target_pairs={{0,2},{1,3},{2,0},{3,1},{4,6},{5,7},{6,4},{7,5},{8,10},{9,11},{10,... | collective-permute-start | bytes 98312 | tf_op jit(solution)/shard_map/ppermute | solution.py:177
  80.2 2.6 %collective-permute-start.5 = (f32[4,16,128]{2,1,0:T(8,128)S(1)}, f32[4,16,128]{2,1,0:T(8,128)S(1)}, u32[]{:S(2)}, u32[]{:S(2)}) collective-permute-start(f32[4,16,128]{2,1,0:T(8,128)S(1)} %bitcast.106), channel_id=1, source_target_pairs={{0,4},{1,5},{2,6},{3,7},{4,0},{5,1},{6,2},{7,3},{8,12},{9,13},{10,... | collective-permute-start | bytes 98312 | tf_op jit(solution)/shard_map/ppermute | solution.py:177
  82.8 1.6 %collective-permute-start.6 = (f32[4,16,128]{2,1,0:T(8,128)S(1)}, f32[4,16,128]{2,1,0:T(8,128)S(1)}, u32[]{:S(2)}, u32[]{:S(2)}) collective-permute-start(f32[4,16,128]{2,1,0:T(8,128)S(1)} %bitcast.105), channel_id=1, source_target_pairs={{0,5},{1,4},{2,7},{3,6},{4,1},{5,0},{6,3},{7,2},{8,13},{9,12},{10,... | collective-permute-start | bytes 98312 | tf_op jit(solution)/shard_map/ppermute | solution.py:177
  84.4 0.8 copy.57
  85.3 2.3 %reshape.86 = f32[8,1,8192]{2,1,0:T(1,128)} reshape(f32[1024,4,16]{2,1,0:T(4,128)S(1)} %bitcast.91) | data formatting | bytes 524288
  87.6 4.5 %all-to-all-start = ((f32[8,1,8192]{2,1,0:T(1,128)}), f32[8,1,8192]{2,1,0:T(1,128)S(1)}, u32[]{:S(2)}, u32[]{:S(2)}) async-start(f32[8,1,8192]{2,1,0:T(1,128)} %reshape.86), calls=%async_computation | async-start | bytes 524288 | tf_op jit(solution)/shard_map/all_to_all | solution.py:180
  92.0 3.8 %collective-permute-start.7 = (f32[4,16,128]{2,1,0:T(8,128)S(1)}, f32[4,16,128]{2,1,0:T(8,128)S(1)}, u32[]{:S(2)}, u32[]{:S(2)}) collective-permute-start(f32[4,16,128]{2,1,0:T(8,128)S(1)} %bitcast.104), channel_id=1, source_target_pairs={{0,6},{1,7},{2,4},{3,5},{4,2},{5,3},{6,0},{7,1},{8,14},{9,15},{10,... | collective-permute-start | bytes 98312 | tf_op jit(solution)/shard_map/ppermute | solution.py:177
  95.8 1.5 %collective-permute-start.8 = (f32[4,16,128]{2,1,0:T(8,128)S(1)}, f32[4,16,128]{2,1,0:T(8,128)S(1)}, u32[]{:S(2)}, u32[]{:S(2)}) collective-permute-start(f32[4,16,128]{2,1,0:T(8,128)S(1)} %bitcast.103), channel_id=1, source_target_pairs={{0,7},{1,6},{2,5},{3,4},{4,3},{5,2},{6,1},{7,0},{8,15},{9,14},{10,... | collective-permute-start | bytes 98312 | tf_op jit(solution)/shard_map/ppermute | solution.py:177
  97.4 3.0 %collective-permute-done.7 = f32[4,16,128]{2,1,0:T(8,128)S(1)} collective-permute-done((f32[4,16,128]{2,1,0:T(8,128)S(1)}, f32[4,16,128]{2,1,0:T(8,128)S(1)}, u32[]{:S(2)}, u32[]{:S(2)}) %collective-permute-start.7) | collective-permute-done | bytes 32800 | tf_op jit(solution)/shard_map/ppermute | solution.py:177
  100.4 2.2 %collective-permute-done.8 = f32[4,16,128]{2,1,0:T(8,128)S(1)} collective-permute-done((f32[4,16,128]{2,1,0:T(8,128)S(1)}, f32[4,16,128]{2,1,0:T(8,128)S(1)}, u32[]{:S(2)}, u32[]{:S(2)}) %collective-permute-start.8) | collective-permute-done | bytes 32800 | tf_op jit(solution)/shard_map/ppermute | solution.py:177
  102.6 0.6 gather_fusion
  103.2 0.4 reshape_reshape.3
  103.6 0.5 broadcast.209
  104.1 1.3 %reduce = f32[8,8192]{1,0:T(8,128)S(1)} reduce(f32[8,1,8192]{2,1,0:T(1,128)S(1)} %all-to-all-done, f32[]{:T(128)} %broadcast.209), dimensions={1}, to_apply=%all_to_all.11.reduce_sub_computation | reduce | bytes 524292 | tf_op jit(solution)/shard_map/all_to_all | solution.py:180
  105.4 1.5 %reshape.87 = f32[1024,4,16]{2,1,0:T(4,128)S(1)} reshape(f32[8,8192]{1,0:T(8,128)S(1)} %reduce) | data formatting | bytes 524288
  106.9 0.8 copy.58
  107.7 0.5 reshape.68
  108.4 0.9 convolution_bitcast_fusion.2
  109.3 1.0 convolution_bitcast_fusion.1
  110.5 10.5 %psum.7 = f32[20,4,128]{2,1,0:T(4,128)S(1)} all-reduce(f32[20,4,128]{2,1,0:T(4,128)S(1)} %copy.74), channel_id=1, replica_groups=mesh['inl'=4,'xl'=8] {'inl'}, use_global_device_ids=true, to_apply=%region_3.4 | all-reduce | flops 10240 | bytes 81920 | tf_op jit(solution)/shard_map/psum | solution.py:189
  121.3 0.6 pad_maximum_fusion.3
  (282 shorter events, 54.1 us)
Async XLA Ops:
  0.6 13.0 %copy-start.1 = (f32[4,16,1024]{2,1,0:T(8,128)S(1)}, f32[4,16,1024]{2,1,0:T(8,128)}, u32[]{:S(2)}) copy-start(f32[4,16,1024]{2,1,0:T(8,128)} %param.7) | copy-start | bytes 786436
  0.6 13.0 %copy-start = (f32[4,16,1024]{2,1,0:T(8,128)S(1)}, f32[4,16,1024]{2,1,0:T(8,128)}, u32[]{:S(2)}) copy-start(f32[4,16,1024]{2,1,0:T(8,128)} %param.8) | copy-start | bytes 786436
  1.9 9.9 %collective-permute-start = (f32[2,4,3,1024]{3,2,1,0:T(4,128)S(1)}, f32[2,4,3,1024]{3,2,1,0:T(4,128)S(1)}, u32[]{:S(2)}, u32[]{:S(2)}) collective-permute-start(f32[2,4,3,1024]{3,2,1,0:T(4,128)S(1)} %get-tuple-element.486), channel_id=1, source_target_pairs={{0,1},{1,2},{2,3},{3,4},{4,5},{5,6},{6,7},{8,9},{9,10},{10,11},{11... | collective-permute-start | bytes 294920 | tf_op jit(solution)/shard_map/ppermute | solution.py:33
  6.7 6.9 %collective-permute-start.1 = (f32[2,4,3,1024]{3,2,1,0:T(4,128)S(1)}, f32[2,4,3,1024]{3,2,1,0:T(4,128)S(1)}, u32[]{:S(2)}, u32[]{:S(2)}) collective-permute-start(f32[2,4,3,1024]{3,2,1,0:T(4,128)S(1)} %get-tuple-element.487), channel_id=1, source_target_pairs={{1,0},{2,1},{3,2},{4,3},{5,4},{6,5},{7,6},{9,8},{10,9},{11,10},{12... | collective-permute-start | bytes 294920 | tf_op jit(solution)/shard_map/ppermute | solution.py:36
  76.1 15.9 %collective-permute-start.2 = (f32[4,16,128]{2,1,0:T(8,128)S(1)}, f32[4,16,128]{2,1,0:T(8,128)S(1)}, u32[]{:S(2)}, u32[]{:S(2)}) collective-permute-start(f32[4,16,128]{2,1,0:T(8,128)S(1)} %bitcast.109), channel_id=1, source_target_pairs={{0,1},{1,0},{2,3},{3,2},{4,5},{5,4},{6,7},{7,6},{8,9},{9,8},{10,11... | collective-permute-start | bytes 98312 | tf_op jit(solution)/shard_map/ppermute | solution.py:177
  78.6 17.3 %collective-permute-start.3 = (f32[4,16,128]{2,1,0:T(8,128)S(1)}, f32[4,16,128]{2,1,0:T(8,128)S(1)}, u32[]{:S(2)}, u32[]{:S(2)}) collective-permute-start(f32[4,16,128]{2,1,0:T(8,128)S(1)} %bitcast.108), channel_id=1, source_target_pairs={{0,2},{1,3},{2,0},{3,1},{4,6},{5,7},{6,4},{7,5},{8,10},{9,11},{10,... | collective-permute-start | bytes 98312 | tf_op jit(solution)/shard_map/ppermute | solution.py:177
  80.2 17.1 %collective-permute-start.4 = (f32[4,16,128]{2,1,0:T(8,128)S(1)}, f32[4,16,128]{2,1,0:T(8,128)S(1)}, u32[]{:S(2)}, u32[]{:S(2)}) collective-permute-start(f32[4,16,128]{2,1,0:T(8,128)S(1)} %bitcast.107), channel_id=1, source_target_pairs={{0,3},{1,2},{2,1},{3,0},{4,7},{5,6},{6,5},{7,4},{8,11},{9,10},{10,... | collective-permute-start | bytes 98312 | tf_op jit(solution)/shard_map/ppermute | solution.py:177
  80.2 17.2 %collective-permute-start.5 = (f32[4,16,128]{2,1,0:T(8,128)S(1)}, f32[4,16,128]{2,1,0:T(8,128)S(1)}, u32[]{:S(2)}, u32[]{:S(2)}) collective-permute-start(f32[4,16,128]{2,1,0:T(8,128)S(1)} %bitcast.106), channel_id=1, source_target_pairs={{0,4},{1,5},{2,6},{3,7},{4,0},{5,1},{6,2},{7,3},{8,12},{9,13},{10,... | collective-permute-start | bytes 98312 | tf_op jit(solution)/shard_map/ppermute | solution.py:177
  82.8 14.6 %collective-permute-start.6 = (f32[4,16,128]{2,1,0:T(8,128)S(1)}, f32[4,16,128]{2,1,0:T(8,128)S(1)}, u32[]{:S(2)}, u32[]{:S(2)}) collective-permute-start(f32[4,16,128]{2,1,0:T(8,128)S(1)} %bitcast.105), channel_id=1, source_target_pairs={{0,5},{1,4},{2,7},{3,6},{4,1},{5,0},{6,3},{7,2},{8,13},{9,12},{10,... | collective-permute-start | bytes 98312 | tf_op jit(solution)/shard_map/ppermute | solution.py:177
  87.6 16.1 %all-to-all-start = ((f32[8,1,8192]{2,1,0:T(1,128)}), f32[8,1,8192]{2,1,0:T(1,128)S(1)}, u32[]{:S(2)}, u32[]{:S(2)}) async-start(f32[8,1,8192]{2,1,0:T(1,128)} %reshape.86), calls=%async_computation | async-start | bytes 524288 | tf_op jit(solution)/shard_map/all_to_all | solution.py:180
  92.0 8.4 %collective-permute-start.7 = (f32[4,16,128]{2,1,0:T(8,128)S(1)}, f32[4,16,128]{2,1,0:T(8,128)S(1)}, u32[]{:S(2)}, u32[]{:S(2)}) collective-permute-start(f32[4,16,128]{2,1,0:T(8,128)S(1)} %bitcast.104), channel_id=1, source_target_pairs={{0,6},{1,7},{2,4},{3,5},{4,2},{5,3},{6,0},{7,1},{8,14},{9,15},{10,... | collective-permute-start | bytes 98312 | tf_op jit(solution)/shard_map/ppermute | solution.py:177
  95.8 6.7 %collective-permute-start.8 = (f32[4,16,128]{2,1,0:T(8,128)S(1)}, f32[4,16,128]{2,1,0:T(8,128)S(1)}, u32[]{:S(2)}, u32[]{:S(2)}) collective-permute-start(f32[4,16,128]{2,1,0:T(8,128)S(1)} %bitcast.103), channel_id=1, source_target_pairs={{0,7},{1,6},{2,5},{3,4},{4,3},{5,2},{6,1},{7,0},{8,15},{9,14},{10,... | collective-permute-start | bytes 98312 | tf_op jit(solution)/shard_map/ppermute | solution.py:177
